TPU v7x, 256 devices: a whole 4x4x8 slice. The times are simulated.
256 devices in a mesh: own: 2 (over y_hi), space: 128 (over z, x, y_lo, core).
Axes of the slice: x: 4, y: 4 (y_hi: 2, y_lo: 2; y = y_hi * 2 + y_lo), z: 8, core: 2. Of those that a mesh axis runs over, the one named last changes fastest.
Arguments:
- density: bfloat16 [256, 4, 512, 128], P(None, 'own', 'space'), may hold values from -6 to 6
- cotangent: bfloat16 [256, 4, 512, 128], P(None, 'own', 'space'), may hold values from -6 to 6
- pw_one: bfloat16 [256, 256], P('own'), may hold values from -0.375 to 0.375
- pw_two: bfloat16 [256, 256], P('own'), may hold values from -0.375 to 0.375
- dw_one: bfloat16 [27, 256], P(None, 'own'), may hold values from -1.25 to 1.25
- dw_two: bfloat16 [27, 256], P(None, 'own'), may hold values from -1.25 to 1.25
Outputs:
- grad_input: bfloat16 [256, 4, 512, 128], P(None, 'own', 'space')
- grad_pw_one: float32 [256, 256], P('own')
- grad_pw_two: float32 [256, 256], P('own')
- grad_dw_one: float32 [27, 256], P(None, 'own')
- grad_dw_two: float32 [27, 256], P(None, 'own')
All inputs are finite; a program needn't handle non-finite values.
Results may differ from a plain program's by a relative error of at most 0.01.
Values may be sent and summed in bfloat16 or wider, within the bound.
A program may use at most 192 MiB of HBM per device.

v0:
```python
import math
import jax
import jax.numpy as jnp
from jax import lax
from jax.sharding import PartitionSpec as P

TAP_LIST = [
    (9 * (a + 1) + 3 * (b + 1) + (d + 1), a, b, d)
    for a in (-1, 0, 1)
    for b in (-1, 0, 1)
    for d in (-1, 0, 1)
]


def extended(value, sides, width):
    for axis, dim in sides:
        size, length = (lax.axis_size(axis), value.shape[dim])
        up = [(i, (i + 1) % size) for i in range(size)]
        down = [(j, i) for i, j in up]
        last = lax.slice_in_dim(value, length - width, length, axis=dim)
        first = lax.slice_in_dim(value, 0, width, axis=dim)
        before = lax.ppermute(last, axis, up)
        after = lax.ppermute(first, axis, down)
        value = jnp.concatenate([before, value, after], axis=dim)
    return value


def depthwise(padded, weights, extent_x, extent_y, direction):
    running = jnp.zeros((padded.shape[0], extent_x, extent_y, padded.shape[3]), jnp.float32)
    for k, a, b, d in TAP_LIST:
        start_x = 1 + direction * a
        start_y = 1 + direction * b
        shifted = padded[:, start_x : start_x + extent_x, start_y : start_y + extent_y, :]
        shifted = jnp.roll(shifted, -direction * d, axis=3).astype(jnp.float32)
        running = running + weights[k].astype(jnp.float32)[:, None, None, None] * shifted
    return running


def tap_sums(padded, gradient):
    extent_x = gradient.shape[1]
    extent_y = gradient.shape[2]
    grad_float = gradient.astype(jnp.float32)
    columns = []
    for k, a, b, d in TAP_LIST:
        shifted = padded[:, 1 + a : 1 + a + extent_x, 1 + b : 1 + b + extent_y, :]
        shifted = jnp.roll(shifted, -d, axis=3).astype(jnp.float32)
        columns.append(jnp.sum(shifted * grad_float, axis=(1, 2, 3)))
    return jnp.stack(columns, axis=0)


def pointwise(weights, source):
    layout = source.shape
    flattened = source.reshape(layout[0], -1)
    return jnp.dot(weights.T, flattened, preferred_element_type=jnp.float32).reshape(layout)


def backmap(weights, source):
    layout = source.shape
    flattened = source.reshape(layout[0], -1)
    return jnp.dot(weights, flattened, preferred_element_type=jnp.float32).reshape(layout)


def contract_cells(left, right):
    channels = left.shape[0]
    return lax.dot_general(
        left.reshape(channels, -1),
        right.reshape(channels, -1),
        (((1,), (1,)), ((), ())),
        preferred_element_type=jnp.float32,
    )


def shards(density, cotangent, pw_one, pw_two, dw_one, dw_two):
    channels, extent_x, extent_y, extent_z = density.shape
    weight_one, weight_two, taps_one, taps_two = (
        lax.all_gather(pw_one, "own", axis=0, tiled=True),
        lax.all_gather(pw_two, "own", axis=0, tiled=True),
        lax.all_gather(dw_one, "own", axis=1, tiled=True),
        lax.all_gather(dw_two, "own", axis=1, tiled=True),
    )
    rim_width = 1
    wide_input = extended(density, (("own", 1), ("space", 2)), rim_width)
    first = depthwise(wide_input, taps_one, extent_x, extent_y, 1).astype(jnp.bfloat16)
    pre = pointwise(weight_one, first)
    act = jax.nn.silu(pre).astype(jnp.bfloat16)
    act_padded = extended(act, (("own", 1), ("space", 2)), 1)
    second = depthwise(act_padded, taps_two, extent_x, extent_y, 1).astype(jnp.bfloat16)
    grad_second = backmap(weight_two, cotangent).astype(jnp.bfloat16)
    second_padded = extended(grad_second, (("own", 1), ("space", 2)), 1)
    sigma = jax.nn.sigmoid(pre)
    grad_pre = (
        depthwise(second_padded, taps_two, extent_x, extent_y, -1)
        * (sigma * (1.0 + pre * (1.0 - sigma)))
    ).astype(jnp.bfloat16)
    grad_first = backmap(weight_one, grad_pre).astype(jnp.bfloat16)
    first_padded = extended(grad_first, (("own", 1), ("space", 2)), 1)
    grad_input = (
        cotangent.astype(jnp.float32) + depthwise(first_padded, taps_one, extent_x, extent_y, -1)
    ).astype(jnp.bfloat16)
    total_cells = extent_x * extent_y * extent_z * lax.axis_size("own") * lax.axis_size("space")
    grad_scale = 1.0 / math.sqrt(float(total_cells))
    local_pw_one = contract_cells(first, grad_pre) * grad_scale
    local_pw_two = contract_cells(second, cotangent) * grad_scale
    local_dw_one = tap_sums(wide_input, grad_first) * grad_scale
    local_dw_two = tap_sums(act_padded, grad_second) * grad_scale
    partials = (local_pw_one, local_pw_two, local_dw_one, local_dw_two)
    summed = lax.psum((partials[0], partials[1], partials[2], partials[3]), ("own", "space"))
    share_rows = channels // lax.axis_size("own")
    position = lax.axis_index("own") * share_rows
    result = (
        lax.dynamic_slice_in_dim(summed[0], position, share_rows, 0),
        lax.dynamic_slice_in_dim(summed[1], position, share_rows, 0),
        lax.dynamic_slice_in_dim(summed[2], position, share_rows, 1),
        lax.dynamic_slice_in_dim(summed[3], position, share_rows, 1),
    )
    return (grad_input, result[0], result[1], result[2], result[3])


def solution(mesh):
    in_specs = (
        P(None, "own", "space", None),
        P(None, "own", "space", None),
        P("own", None),
        P("own", None),
        P(None, "own"),
        P(None, "own"),
    )
    out_specs = (
        P(None, "own", "space", None),
        P("own", None),
        P("own", None),
        P(None, "own"),
        P(None, "own"),
    )
    return jax.shard_map(shards, mesh=mesh, in_specs=in_specs, out_specs=out_specs, check_vma=False)
```

profile of v0, /device:TPU:1, one launch (start us, length us, event | category | flops | bytes accessed | tf_op | source)
XLA Modules:
  0.0 458.6 jit_solution(16944286519748687142)
XLA Ops:
  7.3 1.4 copy.90
  8.7 3.8 collective-permute-start.5
  12.6 11.0 %all_gather.12 = bf16[27,256]{1,0:T(8,128)(2,1)S(1)} all-gather(bf16[27,128]{1,0:T(8,128)(2,1)S(1)} %copy-done.80), channel_id=1, replica_groups=mesh['own'=2,'space'=128] {'own'}, dimensions={1}, use_global_device_ids=true | all-gather | bytes 20736 | tf_op jit(solution)/shard_map/all_gather | solution.py:78
  23.6 0.7 slice_convert_fusion.53
  24.9 5.3 %all_gather.13 = bf16[27,256]{1,0:T(8,128)(2,1)S(1)} all-gather(bf16[27,128]{1,0:T(8,128)(2,1)S(1)} %copy-done.81), channel_id=1, replica_groups=mesh['own'=2,'space'=128] {'own'}, dimensions={1}, use_global_device_ids=true | all-gather | bytes 20736 | tf_op jit(solution)/shard_map/all_gather | solution.py:79
  30.2 0.7 slice_convert_fusion.52
  31.5 5.3 %all_gather.15 = bf16[256,256]{1,0:T(8,128)(2,1)S(1)} all-gather(bf16[128,256]{1,0:T(8,128)(2,1)S(1)} %copy-done.24), channel_id=1, replica_groups=mesh['own'=2,'space'=128] {'own'}, dimensions={0}, use_global_device_ids=true | all-gather | bytes 196608 | tf_op jit(solution)/shard_map/all_gather | solution.py:76
  37.2 1.1 copy.88
  38.3 1.0 copy.89
  39.3 5.4 %all_gather.14 = bf16[256,256]{1,0:T(8,128)(2,1)} all-gather(bf16[128,256]{1,0:T(8,128)(2,1)S(1)} %copy-done.25), channel_id=1, replica_groups=mesh['own'=2,'space'=128] {'own'}, dimensions={0}, use_global_device_ids=true | all-gather | bytes 196608 | tf_op jit(solution)/shard_map/all_gather | solution.py:77
  45.0 6.1 %collective-permute-start.6 = (bf16[256,4,1,128]{3,0,2,1:T(8,128)(2,1)S(1)}, bf16[256,4,1,128]{3,0,2,1:T(8,128)(2,1)}, u32[]{:S(2)}, u32[]{:S(2)}) collective-permute-start(bf16[256,4,1,128]{3,0,2,1:T(8,128)(2,1)S(1)} %copy.93), channel_id=1, source_target_pairs={{0,1},{1,2},{2,3},{3,4},{4,5},{5,6},{6,7},{7,8},{8,9},{9,10},{10,1... | collective-permute-start | bytes 786440 | tf_op jit(solution)/shard_map/ppermute | solution.py:22
  51.1 0.9 copy.96
  52.0 1.4 fusion.146
  53.4 2.3 fusion.217
  55.8 1.8 copy.94
  57.6 3.4 collective-permute-done.7
  60.9 1.8 copy.97
  62.7 1.2 maximum_maximum_fusion.1
  64.3 1.8 fusion.289
  66.4 11.0 %add_convert_fusion = (bf16[256,2,4,128]{0,3,2,1:T(8,128)(2,1)S(1)}, f32[256,2,4,128]{0,3,2,1:T(8,128)}, f32[256,2,4,128]{0,3,2,1:T(8,128)}, f32[256,2,4,128]{0,...) fusion(bf16[256,2,4,128]{0,3,2,1:T(8,128)(2,1)S(1)} %copy.90, ...), kind=kLoop, calls=%fused_computation.272 | loop fusion | flops 57933824 | bytes 27225088 | tf_op jit(solution)/shard_map/convert_element_type | solution.py:83
  78.7 2.6 collective-permute-start.13
  81.3 0.8 collective-permute-start.12
  82.1 1.5 maximum_convert_fusion
  83.7 2.8 collective-permute-done.13
  86.5 5.6 %collective-permute-done.12 = bf16[256,1,4,128]{0,3,2,1:T(8,128)(2,1)S(1)} collective-permute-done((bf16[256,1,4,128]{0,3,2,1:T(8,128)(2,1)S(1)}, bf16[256,1,4,128]{0,3,2,1:T(8,128)(2,1)S(1)}, u32[]{:S(2)}, u32[]{:S(2)}) %collective-permute-start.12) | collective-permute-done | bytes 262176 | tf_op jit(solution)/shard_map/ppermute | solution.py:22
  92.2 1.5 collective-permute-start.14
  93.7 1.0 collective-permute-start.15
  95.2 1.8 collective-permute-done.14
  97.1 2.5 collective-permute-done.15
  99.8 0.7 fusion.284
  100.8 2.1 fusion.120
  103.0 0.8 fusion.294
  103.8 2.9 collective-permute-start
  106.8 0.7 fusion.283
  107.5 1.4 fusion.135
  108.8 1.3 fusion.131
  110.4 2.1 fusion.136
  112.7 5.8 %fusion = f32[256,256]{1,0:T(8,128)} fusion(bf16[256,2,4,128]{0,3,2,1:T(8,128)(2,1)S(1)} %copy-done.11, bf16[256,2,4,128]{0,3,2,1:T(8,128)(2,1)S(1)} %multiply_convert_fusion, f32[256]{0:T(256)S(1)} %bitcast.317, f32[256]{0:T(256)S(1)} %bitcast.319, f32[256]{0:T(256)S(1)} %bitcast.321, f32[256]{0:T(256)S(1)} %bitcast.323, f32[256]{0:T(256)S(1)} %bitcast.325, ...), kind=kOutput, calls=%fused_computation.119 | convolution fusion | flops 192217088 | bytes 14986240 | tf_op jit(solution)/shard_map/dot_general | solution.py:65
  118.5 1.2 fusion.137
  119.7 5.2 %stack.223 = f32[27,256]{1,0:T(8,128)} concatenate(f32[1,256]{1,0:T(1,128)} %bitcast.379, f32[1,256]{1,0:T(1,128)} %bitcast.306, f32[1,256]{1,0:T(1,128)} %bitcast.380, f32[1,256]{1,0:T(1,128)} %bitcast.309, f32[1,256]{1,0:T(1,128)} %bitcast.381, f32[1,256]{1,0:T(1,128)} %bitcast.310, f32[1,256]{1,0:T(1,128)S(1)} %bitcast.275, f32[1,256]{1,0:T(1,128)} %bitcast.303, ...), dimensions={0} | concatenate | bytes 55296 | tf_op jit(solution)/shard_map/stack | solution.py:48
  125.0 1.4 broadcast_multiply_fusion
  126.4 3.4 collective-permute-start.3
  129.8 2.6 collective-permute-start.2
  132.9 3.0 collective-permute-done.3
  136.2 0.7 fusion.288
  137.2 0.7 fusion.287
  138.4 9.1 %fusion.139 = bf16[256,2,4,128]{0,3,2,1:T(8,128)(2,1)S(1)} fusion(f32[256,2,4,128]{0,3,2,1:T(8,128)S(1)} %bitcast.215, bf16[256,2,4,128]{0,3,2,1:T(8,128)(2,1)S(1)} %get-tuple-element.274, bf16[256,1,4,128]{0,3,2,1:T(8,128)(2,1)S(1)} %collective-permute-done, bf16[256,1,4,128]{0,3,2,1:T(8,128)(2,1)S(1)} %collective-permute-done.1, ...), kind=kLoop, calls=%fused_computation.274 | loop fusion | flops 58982400 | bytes 14666752 | tf_op jit(solution)/shard_map/convert_element_type | solution.py:94
  147.5 0.8 copy-done.17
  148.3 1.1 fusion.1
  149.4 8.2 %fusion.95 = (f32[256]{0:T(256)S(1)}, f32[256]{0:T(256)S(1)}, f32[256]{0:T(256)S(1)}, f32[256]{0:T(256)S(1)}, f32[256]{0:T(256)}, /*index=5*/f32[256]{0:T(256)},...) fusion(f32[256,2,4,128]{0,3,2,1:T(8,128)} %get-tuple-element.96, ...), kind=kOutput, calls=%fused_computation.227 | convolution fusion | flops 144174592 | bytes 20072448 | tf_op jit(solution)/shard_map/dot_general | solution.py:60
  157.6 0.8 fusion.293
  158.4 2.9 collective-permute-start.8
  161.5 2.3 fusion.77
  164.1 87.9 %all-reduce = (f32[27,256]{1,0:T(8,128)S(1)}, f32[27,256]{1,0:T(8,128)S(1)}) all-reduce(f32[27,256]{1,0:T(8,128)S(1)} %broadcast_multiply_fusion.1, f32[27,256]{1,0:T(8,128)S(1)} %copy-done.23), channel_id=1, replica_groups=mesh['own'=2,'space'=128] {'own','space'}, use_global_device_ids=true, to_apply=%region_29.30 | all-reduce | flops 13824 | bytes 110592 | tf_op jit(solution)/shard_map/psum | solution.py:107
  253.2 168.2 %all-reduce.4.cloned.1.call-done = (f32[256,256]{1,0:T(8,128)}, f32[256,256]{1,0:T(8,128)}) async-done(((f32[256,256]{1,0:T(8,128)}, f32[256,256]{1,0:T(8,128)}), (f32[256,256]{1,0:T(8,128)}, f32[256,256]{1,0:T(8,128)})) %all-reduce.4.cloned.1.call-update) | async-done | bytes 524304 | tf_op jit(solution)/shard_map/psum | solution.py:107
  421.4 1.6 constant_dynamic-slice_fusion.3
  423.0 1.6 constant_dynamic-slice_fusion.2
  424.8 3.3 collective-permute-start.11
  428.6 1.6 fusion.152
  430.2 1.2 collective-permute-done.11
  431.5 5.6 %collective-permute-done.10 = bf16[256,4,1,128]{3,0,2,1:T(8,128)(2,1)S(1)} collective-permute-done((bf16[256,4,1,128]{3,0,2,1:T(8,128)(2,1)S(1)}, bf16[256,4,1,128]{3,0,2,1:T(8,128)(2,1)S(1)}, u32[]{:S(2)}, u32[]{:S(2)}) %collective-permute-start.10) | collective-permute-done | bytes 262176 | tf_op jit(solution)/shard_map/ppermute | solution.py:23
  438.4 0.7 fusion.285
  440.0 9.5 %fusion.138 = bf16[256,2,4,128]{0,3,2,1:T(8,128)(2,1)} fusion(bf16[256,2,4,128]{0,3,2,1:T(8,128)(2,1)S(1)} %bitcast.213, bf16[256,2,4,128]{0,3,2,1:T(8,128)(2,1)S(1)} %copy-done.12, bf16[256,1,4,128]{0,3,2,1:T(8,128)(2,1)S(1)} %collective-permute-done.8, bf16[256,1,4,128]{0,3,2,1:T(8,128)(2,1)S(1)} %collective-permute-done.9, ...), kind=kLoop, calls=%fused_computation.273 | loop fusion | flops 57409536 | bytes 14142464 | tf_op jit(solution)/shard_map/convert_element_type | solution.py:99
  449.5 2.1 copy.112
  (344 shorter events, 9.9 us)
Async XLA Ops:
  7.2 5.4 %copy-start.80 = (bf16[27,128]{1,0:T(8,128)(2,1)S(1)}, bf16[27,128]{1,0:T(8,128)(2,1)}, u32[]{:S(2)}) copy-start(bf16[27,128]{1,0:T(8,128)(2,1)} %param.10) | copy-start | bytes 20740
  7.2 17.7 %copy-start.81 = (bf16[27,128]{1,0:T(8,128)(2,1)S(1)}, bf16[27,128]{1,0:T(8,128)(2,1)}, u32[]{:S(2)}) copy-start(bf16[27,128]{1,0:T(8,128)(2,1)} %param.11) | copy-start | bytes 20740
  7.2 24.3 %copy-start.24 = (bf16[128,256]{1,0:T(8,128)(2,1)S(1)}, bf16[128,256]{1,0:T(8,128)(2,1)}, u32[]{:S(2)}) copy-start(bf16[128,256]{1,0:T(8,128)(2,1)} %param.8) | copy-start | bytes 196612
  7.2 29.6 %copy-start.18 = (bf16[256,2,4,128]{3,2,1,0:T(4,128)(2,1)S(1)}, bf16[256,2,4,128]{3,2,1,0:T(4,128)(2,1)}, u32[]{:S(2)}) copy-start(bf16[256,2,4,128]{3,2,1,0:T(4,128)(2,1)} %param.7) | copy-start | bytes 1572868
  7.2 414.2 %all-reduce.4.cloned.1.call-start = ((), (), s32[]{:S(2)}) async-start(), calls=%async_computation | async-start | bytes 1048576 | tf_op jit(solution)/shard_map/psum | solution.py:107
  8.7 36.1 %collective-permute-start.5 = (bf16[256,1,4,128]{0,3,2,1:T(8,128)(2,1)S(1)}, bf16[256,1,4,128]{0,3,2,1:T(8,128)(2,1)S(1)}, u32[]{:S(2)}, u32[]{:S(2)}) collective-permute-start(bf16[256,1,4,128]{0,3,2,1:T(8,128)(2,1)S(1)} %get-tuple-element.218), channel_id=1, source_target_pairs={{128,0},{0,128},{129,1},{1,129},{130,2},{2,130},{131,3},{3,131},{1... | collective-permute-start | bytes 786440 | tf_op jit(solution)/shard_map/ppermute | solution.py:23
  12.5 32.3 %collective-permute-start.4 = (bf16[256,1,4,128]{0,3,2,1:T(8,128)(2,1)S(1)}, bf16[256,1,4,128]{0,3,2,1:T(8,128)(2,1)S(1)}, u32[]{:S(2)}, u32[]{:S(2)}) collective-permute-start(bf16[256,1,4,128]{0,3,2,1:T(8,128)(2,1)S(1)} %get-tuple-element.217), channel_id=1, source_target_pairs={{0,128},{128,0},{1,129},{129,1},{2,130},{130,2},{3,131},{131,3},{4... | collective-permute-start | bytes 786440 | tf_op jit(solution)/shard_map/ppermute | solution.py:22
  45.0 10.7 %collective-permute-start.6 = (bf16[256,4,1,128]{3,0,2,1:T(8,128)(2,1)S(1)}, bf16[256,4,1,128]{3,0,2,1:T(8,128)(2,1)}, u32[]{:S(2)}, u32[]{:S(2)}) collective-permute-start(bf16[256,4,1,128]{3,0,2,1:T(8,128)(2,1)S(1)} %copy.93), channel_id=1, source_target_pairs={{0,1},{1,2},{2,3},{3,4},{4,5},{5,6},{6,7},{7,8},{8,9},{9,10},{10,1... | collective-permute-start | bytes 786440 | tf_op jit(solution)/shard_map/ppermute | solution.py:22
  52.0 8.9 %collective-permute-start.7 = (bf16[256,4,1,128]{3,0,2,1:T(8,128)(2,1)}, bf16[256,4,1,128]{3,0,2,1:T(8,128)(2,1)}, u32[]{:S(2)}, u32[]{:S(2)}) collective-permute-start(bf16[256,4,1,128]{3,0,2,1:T(8,128)(2,1)} %copy.96), channel_id=1, source_target_pairs={{1,0},{2,1},{3,2},{4,3},{5,4},{6,5},{7,6},{8,7},{9,8},{10,9},{11,1... | collective-permute-start | bytes 786440 | tf_op jit(solution)/shard_map/ppermute | solution.py:23
  53.4 2.3 copy-start.3
  53.4 2.3 copy-start.5
  78.7 7.8 %collective-permute-start.13 = (bf16[256,1,4,128]{0,3,2,1:T(8,128)(2,1)S(1)}, bf16[256,1,4,128]{0,3,2,1:T(8,128)(2,1)S(1)}, u32[]{:S(2)}, u32[]{:S(2)}) collective-permute-start(bf16[256,1,4,128]{0,3,2,1:T(8,128)(2,1)S(1)} %get-tuple-element.190), channel_id=1, source_target_pairs={{128,0},{0,128},{129,1},{1,129},{130,2},{2,130},{131,3},{3,131},{1... | collective-permute-start | bytes 786440 | tf_op jit(solution)/shard_map/ppermute | solution.py:23
  81.3 10.8 %collective-permute-start.12 = (bf16[256,1,4,128]{0,3,2,1:T(8,128)(2,1)S(1)}, bf16[256,1,4,128]{0,3,2,1:T(8,128)(2,1)S(1)}, u32[]{:S(2)}, u32[]{:S(2)}) collective-permute-start(bf16[256,1,4,128]{0,3,2,1:T(8,128)(2,1)S(1)} %get-tuple-element.189), channel_id=1, source_target_pairs={{0,128},{128,0},{1,129},{129,1},{2,130},{130,2},{3,131},{131,3},{4... | collective-permute-start | bytes 786440 | tf_op jit(solution)/shard_map/ppermute | solution.py:22
  92.2 4.9 %collective-permute-start.14 = (bf16[256,4,1,128]{0,3,2,1:T(8,128)(2,1)S(1)}, bf16[256,4,1,128]{0,3,2,1:T(8,128)(2,1)S(1)}, u32[]{:S(2)}, u32[]{:S(2)}) collective-permute-start(bf16[256,4,1,128]{0,3,2,1:T(8,128)(2,1)S(1)} %get-tuple-element.147), channel_id=1, source_target_pairs={{0,1},{1,2},{2,3},{3,4},{4,5},{5,6},{6,7},{7,8},{8,9},{9,10},{10,1... | collective-permute-start | bytes 786440 | tf_op jit(solution)/shard_map/ppermute | solution.py:22
  93.7 5.8 %collective-permute-start.15 = (bf16[256,4,1,128]{0,3,2,1:T(8,128)(2,1)S(1)}, bf16[256,4,1,128]{0,3,2,1:T(8,128)(2,1)S(1)}, u32[]{:S(2)}, u32[]{:S(2)}) collective-permute-start(bf16[256,4,1,128]{0,3,2,1:T(8,128)(2,1)S(1)} %get-tuple-element.148), channel_id=1, source_target_pairs={{1,0},{2,1},{3,2},{4,3},{5,4},{6,5},{7,6},{8,7},{9,8},{10,9},{11,1... | collective-permute-start | bytes 786440 | tf_op jit(solution)/shard_map/ppermute | solution.py:23
  103.8 22.5 %collective-permute-start = (bf16[256,1,4,128]{0,3,2,1:T(8,128)(2,1)}, bf16[256,1,4,128]{0,3,2,1:T(8,128)(2,1)S(1)}, u32[]{:S(2)}, u32[]{:S(2)}) collective-permute-start(bf16[256,1,4,128]{0,3,2,1:T(8,128)(2,1)} %get-tuple-element.210), channel_id=1, source_target_pairs={{0,128},{128,0},{1,129},{129,1},{2,130},{130,2},{3,131},{131,3},{4... | collective-permute-start | bytes 786440 | tf_op jit(solution)/shard_map/ppermute | solution.py:22
  106.7 19.6 %collective-permute-start.1 = (bf16[256,1,4,128]{0,3,2,1:T(8,128)(2,1)}, bf16[256,1,4,128]{0,3,2,1:T(8,128)(2,1)S(1)}, u32[]{:S(2)}, u32[]{:S(2)}) collective-permute-start(bf16[256,1,4,128]{0,3,2,1:T(8,128)(2,1)} %get-tuple-element.209), channel_id=1, source_target_pairs={{128,0},{0,128},{129,1},{1,129},{130,2},{2,130},{131,3},{3,131},{1... | collective-permute-start | bytes 786440 | tf_op jit(solution)/shard_map/ppermute | solution.py:23
  110.1 2.3 copy-start.100
  110.1 2.3 copy-start.102
  110.2 2.3 copy-start.104
  110.2 2.3 copy-start.106
  110.2 2.3 copy-start.108
  110.2 2.3 copy-start.110
  110.2 2.3 copy-start.112
  110.2 2.3 copy-start.114
  110.2 2.3 copy-start.116
  110.2 2.3 copy-start.118
  110.2 2.3 copy-start.120
  110.2 2.3 copy-start.122
  110.3 2.3 copy-start.124
  110.3 2.3 copy-start.126
  110.3 2.3 copy-start.128
  110.3 2.3 copy-start.130
  110.3 2.3 copy-start.132
  110.3 2.3 copy-start.134
  110.3 2.3 copy-start.136
  110.3 2.3 copy-start.138
  110.3 2.3 copy-start.140
  110.3 2.3 copy-start.142
  110.4 2.3 copy-start.144
  110.4 2.3 copy-start.146
  110.4 2.3 copy-start.148
  126.4 9.6 %collective-permute-start.3 = (bf16[256,4,1,128]{0,3,2,1:T(8,128)(2,1)S(1)}, bf16[256,4,1,128]{0,3,2,1:T(8,128)(2,1)S(1)}, u32[]{:S(2)}, u32[]{:S(2)}) collective-permute-start(bf16[256,4,1,128]{0,3,2,1:T(8,128)(2,1)S(1)} %get-tuple-element.156), channel_id=1, source_target_pairs={{0,1},{1,2},{2,3},{3,4},{4,5},{5,6},{6,7},{7,8},{8,9},{9,10},{10,1... | collective-permute-start | bytes 786440 | tf_op jit(solution)/shard_map/ppermute | solution.py:22
  129.8 6.1 %collective-permute-start.2 = (bf16[256,4,1,128]{0,3,2,1:T(8,128)(2,1)S(1)}, bf16[256,4,1,128]{0,3,2,1:T(8,128)(2,1)S(1)}, u32[]{:S(2)}, u32[]{:S(2)}) collective-permute-start(bf16[256,4,1,128]{0,3,2,1:T(8,128)(2,1)S(1)} %get-tuple-element.155), channel_id=1, source_target_pairs={{1,0},{2,1},{3,2},{4,3},{5,4},{6,5},{7,6},{8,7},{9,8},{10,9},{11,1... | collective-permute-start | bytes 786440 | tf_op jit(solution)/shard_map/ppermute | solution.py:23
  138.4 9.9 %copy-start.20 = (bf16[256,2,4,128]{0,3,2,1:T(8,128)(2,1)S(1)}, bf16[256,2,4,128]{0,3,2,1:T(8,128)(2,1)}, u32[]{:S(2)}) copy-start(bf16[256,2,4,128]{0,3,2,1:T(8,128)(2,1)} %copy-done.19) | copy-start | bytes 1572868
  158.4 266.2 %collective-permute-start.8 = (bf16[256,1,4,128]{0,3,2,1:T(8,128)(2,1)}, bf16[256,1,4,128]{0,3,2,1:T(8,128)(2,1)S(1)}, u32[]{:S(2)}, u32[]{:S(2)}) collective-permute-start(bf16[256,1,4,128]{0,3,2,1:T(8,128)(2,1)} %get-tuple-element.200), channel_id=1, source_target_pairs={{0,128},{128,0},{1,129},{129,1},{2,130},{130,2},{3,131},{131,3},{4... | collective-permute-start | bytes 786440 | tf_op jit(solution)/shard_map/ppermute | solution.py:22
  161.3 263.2 %collective-permute-start.9 = (bf16[256,1,4,128]{0,3,2,1:T(8,128)(2,1)}, bf16[256,1,4,128]{0,3,2,1:T(8,128)(2,1)S(1)}, u32[]{:S(2)}, u32[]{:S(2)}) collective-permute-start(bf16[256,1,4,128]{0,3,2,1:T(8,128)(2,1)} %get-tuple-element.199), channel_id=1, source_target_pairs={{128,0},{0,128},{129,1},{1,129},{130,2},{2,130},{131,3},{3,131},{1... | collective-permute-start | bytes 786440 | tf_op jit(solution)/shard_map/ppermute | solution.py:23
  161.4 2.4 copy-start.82
  161.4 2.4 copy-start.83
  161.4 2.4 copy-start.84
  161.4 2.4 copy-start.85
  161.4 2.4 copy-start.86
  161.4 2.4 copy-start.87
  161.4 2.4 copy-start.88
  161.5 2.4 copy-start.89
  161.5 2.4 copy-start.90
  161.5 2.4 copy-start.91
  161.5 2.4 copy-start.92
  161.5 2.4 copy-start.93
  161.5 2.4 copy-start.94
  161.5 2.4 copy-start.95
  161.5 2.5 copy-start.23
  424.8 6.6 %collective-permute-start.11 = (bf16[256,4,1,128]{3,0,2,1:T(8,128)(2,1)S(1)}, bf16[256,4,1,128]{3,0,2,1:T(8,128)(2,1)S(1)}, u32[]{:S(2)}, u32[]{:S(2)}) collective-permute-start(bf16[256,4,1,128]{3,0,2,1:T(8,128)(2,1)S(1)} %copy.106), channel_id=1, source_target_pairs={{0,1},{1,2},{2,3},{3,4},{4,5},{5,6},{6,7},{7,8},{8,9},{9,10},{10,1... | collective-permute-start | bytes 786440 | tf_op jit(solution)/shard_map/ppermute | solution.py:22
  428.2 8.9 %collective-permute-start.10 = (bf16[256,4,1,128]{3,0,2,1:T(8,128)(2,1)S(1)}, bf16[256,4,1,128]{3,0,2,1:T(8,128)(2,1)S(1)}, u32[]{:S(2)}, u32[]{:S(2)}) collective-permute-start(bf16[256,4,1,128]{3,0,2,1:T(8,128)(2,1)S(1)} %copy.104), channel_id=1, source_target_pairs={{1,0},{2,1},{3,2},{4,3},{5,4},{6,5},{7,6},{8,7},{9,8},{10,9},{11,1... | collective-permute-start | bytes 786440 | tf_op jit(solution)/shard_map/ppermute | solution.py:23
  (103 other events, 170.5 us)
Sparse Core Ops, SparseCore 0:
  161.5 259.8 all-reduce.3
where the time goes:
time: 468 us; the launch traced here: 459 us
  waiting for transfers between devices  194 us (41%)
  blocking collectives  115 us (25%)
  other arithmetic  52.1 us (11%)
  local copies, waits for them, and re-layouts  31.8 us (7%)
  starting transfers between devices  31.6 us (7%)
  matrix products  17.5 us (4%)
  between operations  16.6 us (4%)
    psum x1, waiting for transfers between devices, shards(): lax.psum((partials[0], partials[1], partials[2], partials[3]), ('own', 's...  168 us
    psum x1, blocking collectives, shards(): lax.psum((partials[0], partials[1], partials[2], partials[3]), ('own', 's...  87.9 us
    ppermute x8, starting transfers between devices, extended(): before = lax.ppermute(last, axis, up)  21.1 us
    ppermute x8, waiting for transfers between devices, extended(): after = lax.ppermute(first, axis, down)  14.3 us
    ppermute x8, waiting for transfers between devices, extended(): before = lax.ppermute(last, axis, up)  11.7 us
    convert_element_type x1, other arithmetic, shards(): depthwise(wide_input, taps_one, extent_x, extent_y, 1).astype(jnp.bfloat16)  11 us
    all_gather x1, blocking collectives, shards(): lax.all_gather(dw_one, 'own', axis=1, tiled=True)  11 us
    ppermute x8, starting transfers between devices, extended(): after = lax.ppermute(first, axis, down)  10.5 us
  transfers between devices with their start and end apart: 17, of which 9 were waited for; matrix products, arithmetic and copies ran while one was open for 9% of the time, Pallas kernels for 0%

commit v1 on v0

--- a/solution.py
+++ b/solution.py
@@ -3,6 +3,7 @@
 import jax.numpy as jnp
 from jax import lax
 from jax.sharding import PartitionSpec as P
+from jax.lax import psum
 
 TAP_LIST = [
     (9 * (a + 1) + 3 * (b + 1) + (d + 1), a, b, d)
@@ -104,7 +105,9 @@
     local_dw_one = tap_sums(wide_input, grad_first) * grad_scale
     local_dw_two = tap_sums(act_padded, grad_second) * grad_scale
     partials = (local_pw_one, local_pw_two, local_dw_one, local_dw_two)
-    summed = lax.psum((partials[0], partials[1], partials[2], partials[3]), ("own", "space"))
+    summed = (partials[0], partials[1], partials[2], partials[3])
+    for tick in ("space", "own"):
+        summed = psum(summed, tick)
     share_rows = channels // lax.axis_size("own")
     position = lax.axis_index("own") * share_rows
     result = (

time: 468 us -> 1240 us (2.65)
  blocking collectives: 115 us -> 592 us
  waiting for transfers between devices: 194 us -> 472 us
    psum x1 -> x2, blocking collectives: 87.9 us -> 565 us  [shards(): summed = psum(summed, tick)]
    psum x1 -> x2, waiting for transfers between devices: 168 us -> 452 us  [shards(): summed = psum(summed, tick)]
  transfers between devices with their start and end apart: 17 -> 18, of which waited for: 9 -> 8; matrix products, arithmetic and copies ran while one was open for 9% -> 5% of each run, Pallas kernels for 0% -> 0%
where the time goes in v1:
time: 1240 us; the launch traced here: 1230 us
  blocking collectives  592 us (48%)
  waiting for transfers between devices  472 us (38%)
  other arithmetic  53.8 us (4%)
  starting transfers between devices  39.5 us (3%)
  local copies, waits for them, and re-layouts  35.4 us (3%)
  matrix products  17.5 us (1%)
  between operations  16.5 us (1%)
    psum x2, blocking collectives, shards(): summed = psum(summed, tick)  565 us
    psum x2, waiting for transfers between devices, shards(): summed = psum(summed, tick)  452 us
  transfers between devices with their start and end apart: 18, of which 8 were waited for; matrix products, arithmetic and copies ran while one was open for 5% of the time, Pallas kernels for 0%

profile of v1, /device:TPU:1, one launch (start us, length us, event | category | flops | bytes accessed | tf_op | source)
XLA Modules:
  0.0 1226.2 jit_solution(14830420615026591437)
XLA Ops:
  7.3 1.4 copy.90
  8.7 3.8 collective-permute-start.5
  12.6 11.0 all_gather.12
  24.9 5.4 all_gather.13
  31.5 5.3 all_gather.15
  37.2 1.1 copy.88
  38.3 1.0 copy.89
  39.3 5.4 all_gather.14
  45.0 6.1 collective-permute-start.6
  51.1 0.8 copy.96
  52.0 1.4 fusion.146
  53.4 2.3 fusion.217
  55.7 1.8 copy.94
  57.5 3.4 collective-permute-done.7
  60.9 1.8 copy.97
  62.7 1.2 maximum_maximum_fusion.1
  64.3 1.8 fusion.289
  66.4 11.0 add_convert_fusion
  78.7 2.6 collective-permute-start.13
  81.3 0.8 collective-permute-start.12
  82.1 1.6 maximum_convert_fusion
  83.7 2.9 collective-permute-done.13
  86.5 5.6 collective-permute-done.12
  92.2 1.5 collective-permute-start.14
  93.7 1.0 collective-permute-start.15
  95.2 1.8 collective-permute-done.14
  97.0 2.5 collective-permute-done.15
  100.8 2.2 fusion.120
  103.0 0.8 fusion.294
  103.8 2.9 collective-permute-start
  107.5 1.4 fusion.135
  108.9 1.3 fusion.131
  110.4 2.1 fusion.136
  112.7 5.8 fusion
  118.5 1.2 fusion.137
  119.7 5.3 stack.223
  125.0 1.4 broadcast_multiply_fusion
  126.4 3.4 collective-permute-start.3
  129.9 2.6 collective-permute-start.2
  132.9 3.0 collective-permute-done.3
  137.2 0.7 fusion.287
  138.4 9.1 fusion.139
  147.5 0.8 copy-done.14
  148.3 1.0 fusion.1
  149.4 8.3 fusion.95
  157.6 0.8 fusion.293
  158.5 2.9 collective-permute-start.8
  161.6 0.9 fusion.77
  162.9 554.2 %all-reduce = (f32[27,256]{1,0:T(8,128)S(1)}, f32[27,256]{1,0:T(8,128)S(1)}) all-reduce(f32[27,256]{1,0:T(8,128)S(1)} %broadcast_multiply_fusion.1, f32[27,256]{1,0:T(8,128)S(1)} %copy-done.20), channel_id=1, replica_groups=mesh['own'=2,'space'=128] {'space'}, use_global_device_ids=true, to_apply=%region_31.32 | all-reduce | flops 13824 | bytes 110592 | tf_op jit(solution)/shard_map/psum | solution.py:110
  717.0 10.5 all-reduce.2
  729.1 2.4 collective-permute-start.11
  731.6 8.9 collective-permute-start.10
  740.6 1.6 fusion.152
  742.2 0.9 copy.107
  743.1 0.9 copy.105
  744.0 1.4 pad_maximum_fusion.2
  745.4 2.0 fusion.286
  747.6 2.1 fusion.285
  749.7 421.4 %all-reduce.7.cloned.1.call-done = (f32[256,256]{1,0:T(8,128)}, f32[256,256]{1,0:T(8,128)}) async-done(((f32[256,256]{1,0:T(8,128)}, f32[256,256]{1,0:T(8,128)}), (f32[256,256]{1,0:T(8,128)}, f32[256,256]{1,0:T(8,128)})) %all-reduce.7.cloned.1.call-update) | async-done | bytes 524304 | tf_op jit(solution)/shard_map/psum | solution.py:110
  1171.4 11.5 fusion.138
  1182.9 2.1 copy.112
  1185.0 31.0 %all-reduce.9.cloned.1.call-done = (f32[256,256]{1,0:T(8,128)}, f32[256,256]{1,0:T(8,128)}) async-done(((f32[256,256]{1,0:T(8,128)}, f32[256,256]{1,0:T(8,128)}), (f32[256,256]{1,0:T(8,128)}, f32[256,256]{1,0:T(8,128)})) %all-reduce.9.cloned.1.call-update) | async-done | bytes 524304 | tf_op jit(solution)/shard_map/psum | solution.py:110
  1216.0 1.6 constant_dynamic-slice_fusion.3
  1217.5 1.6 constant_dynamic-slice_fusion.2
  (336 shorter events, 11.5 us)
Async XLA Ops:
  7.2 5.4 copy-start.74
  7.2 17.7 %copy-start.75 = (bf16[27,128]{1,0:T(8,128)(2,1)S(1)}, bf16[27,128]{1,0:T(8,128)(2,1)}, u32[]{:S(2)}) copy-start(bf16[27,128]{1,0:T(8,128)(2,1)} %param.11) | copy-start | bytes 20740
  7.2 24.3 %copy-start.21 = (bf16[128,256]{1,0:T(8,128)(2,1)S(1)}, bf16[128,256]{1,0:T(8,128)(2,1)}, u32[]{:S(2)}) copy-start(bf16[128,256]{1,0:T(8,128)(2,1)} %param.8) | copy-start | bytes 196612
  7.2 29.6 %copy-start.15 = (bf16[256,2,4,128]{3,2,1,0:T(4,128)(2,1)S(1)}, bf16[256,2,4,128]{3,2,1,0:T(4,128)(2,1)}, u32[]{:S(2)}) copy-start(bf16[256,2,4,128]{3,2,1,0:T(4,128)(2,1)} %param.7) | copy-start | bytes 1572868
  7.2 1163.9 %all-reduce.7.cloned.1.call-start = ((), (), s32[]{:S(2)}) async-start(), calls=%async_computation | async-start | bytes 1048576 | tf_op jit(solution)/shard_map/psum | solution.py:110
  8.7 36.1 %collective-permute-start.5 = (bf16[256,1,4,128]{0,3,2,1:T(8,128)(2,1)S(1)}, bf16[256,1,4,128]{0,3,2,1:T(8,128)(2,1)S(1)}, u32[]{:S(2)}, u32[]{:S(2)}) collective-permute-start(bf16[256,1,4,128]{0,3,2,1:T(8,128)(2,1)S(1)} %get-tuple-element.222), channel_id=1, source_target_pairs={{128,0},{0,128},{129,1},{1,129},{130,2},{2,130},{131,3},{3,131},{1... | collective-permute-start | bytes 786440 | tf_op jit(solution)/shard_map/ppermute | solution.py:24
  12.5 32.3 %collective-permute-start.4 = (bf16[256,1,4,128]{0,3,2,1:T(8,128)(2,1)S(1)}, bf16[256,1,4,128]{0,3,2,1:T(8,128)(2,1)S(1)}, u32[]{:S(2)}, u32[]{:S(2)}) collective-permute-start(bf16[256,1,4,128]{0,3,2,1:T(8,128)(2,1)S(1)} %get-tuple-element.221), channel_id=1, source_target_pairs={{0,128},{128,0},{1,129},{129,1},{2,130},{130,2},{3,131},{131,3},{4... | collective-permute-start | bytes 786440 | tf_op jit(solution)/shard_map/ppermute | solution.py:23
  45.0 10.7 collective-permute-start.6
  52.0 8.9 collective-permute-start.7
  53.4 2.3 copy-start.5
  53.4 2.3 copy-start.7
  78.7 7.8 collective-permute-start.13
  81.3 10.8 collective-permute-start.12
  92.2 4.8 collective-permute-start.14
  93.7 5.8 collective-permute-start.15
  103.8 22.6 %collective-permute-start = (bf16[256,1,4,128]{0,3,2,1:T(8,128)(2,1)}, bf16[256,1,4,128]{0,3,2,1:T(8,128)(2,1)S(1)}, u32[]{:S(2)}, u32[]{:S(2)}) collective-permute-start(bf16[256,1,4,128]{0,3,2,1:T(8,128)(2,1)} %get-tuple-element.214), channel_id=1, source_target_pairs={{0,128},{128,0},{1,129},{129,1},{2,130},{130,2},{3,131},{131,3},{4... | collective-permute-start | bytes 786440 | tf_op jit(solution)/shard_map/ppermute | solution.py:23
  106.7 19.7 %collective-permute-start.1 = (bf16[256,1,4,128]{0,3,2,1:T(8,128)(2,1)}, bf16[256,1,4,128]{0,3,2,1:T(8,128)(2,1)S(1)}, u32[]{:S(2)}, u32[]{:S(2)}) collective-permute-start(bf16[256,1,4,128]{0,3,2,1:T(8,128)(2,1)} %get-tuple-element.213), channel_id=1, source_target_pairs={{128,0},{0,128},{129,1},{1,129},{130,2},{2,130},{131,3},{3,131},{1... | collective-permute-start | bytes 786440 | tf_op jit(solution)/shard_map/ppermute | solution.py:24
  110.2 2.3 copy-start.98
  110.2 2.3 copy-start.100
  110.2 2.3 copy-start.102
  110.2 2.3 copy-start.104
  110.2 2.3 copy-start.106
  110.2 2.3 copy-start.108
  110.2 2.3 copy-start.110
  110.2 2.3 copy-start.112
  110.3 2.3 copy-start.114
  110.3 2.3 copy-start.116
  110.3 2.3 copy-start.118
  110.3 2.3 copy-start.120
  110.3 2.3 copy-start.122
  126.4 9.6 collective-permute-start.3
  129.9 6.1 collective-permute-start.2
  138.4 9.9 copy-start.17
  149.4 12.3 %copy-start.1 = (bf16[256,4,5,128]{0,3,2,1:T(8,128)(2,1)S(1)}, bf16[256,4,5,128]{0,3,2,1:T(8,128)(2,1)}, u32[]{:S(2)}) copy-start(bf16[256,4,5,128]{0,3,2,1:T(8,128)(2,1)} %copy-done) | copy-start | bytes 3932164
  158.5 570.4 %collective-permute-start.8 = (bf16[256,1,4,128]{0,3,2,1:T(8,128)(2,1)}, bf16[256,1,4,128]{0,3,2,1:T(8,128)(2,1)S(1)}, u32[]{:S(2)}, u32[]{:S(2)}) collective-permute-start(bf16[256,1,4,128]{0,3,2,1:T(8,128)(2,1)} %get-tuple-element.204), channel_id=1, source_target_pairs={{0,128},{128,0},{1,129},{129,1},{2,130},{130,2},{3,131},{131,3},{4... | collective-permute-start | bytes 786440 | tf_op jit(solution)/shard_map/ppermute | solution.py:23
  161.5 567.3 %collective-permute-start.9 = (bf16[256,1,4,128]{0,3,2,1:T(8,128)(2,1)}, bf16[256,1,4,128]{0,3,2,1:T(8,128)(2,1)S(1)}, u32[]{:S(2)}, u32[]{:S(2)}) collective-permute-start(bf16[256,1,4,128]{0,3,2,1:T(8,128)(2,1)} %get-tuple-element.203), channel_id=1, source_target_pairs={{128,0},{0,128},{129,1},{1,129},{130,2},{2,130},{131,3},{3,131},{1... | collective-permute-start | bytes 786440 | tf_op jit(solution)/shard_map/ppermute | solution.py:24
  162.8 1053.2 %all-reduce.9.cloned.1.call-start = ((), (), s32[]{:S(2)}) async-start(), calls=%async_computation.1 | async-start | bytes 1048576 | tf_op jit(solution)/shard_map/psum | solution.py:110
  728.8 13.4 %copy-start.4 = (bf16[256,1,4,128]{0,3,2,1:T(8,128)(2,1)}, bf16[256,1,4,128]{0,3,2,1:T(8,128)(2,1)S(1)}, u32[]{:S(2)}) copy-start(bf16[256,1,4,128]{0,3,2,1:T(8,128)(2,1)S(1)} %collective-permute-done.9) | copy-start | bytes 786436
  729.1 13.2 %collective-permute-start.11 = (bf16[256,4,1,128]{3,0,2,1:T(8,128)(2,1)S(1)}, bf16[256,4,1,128]{3,0,2,1:T(8,128)(2,1)S(1)}, u32[]{:S(2)}, u32[]{:S(2)}) collective-permute-start(bf16[256,4,1,128]{3,0,2,1:T(8,128)(2,1)S(1)} %copy.106), channel_id=1, source_target_pairs={{0,1},{1,2},{2,3},{3,4},{4,5},{5,6},{6,7},{7,8},{8,9},{9,10},{10,1... | collective-permute-start | bytes 786440 | tf_op jit(solution)/shard_map/ppermute | solution.py:23
  731.6 11.4 collective-permute-start.10
  747.4 423.7 %copy-start.24 = (f32[1,256]{1,0:T(1,128)S(1)}, f32[1,256]{1,0:T(1,128)}, u32[]{:S(2)}) copy-start(f32[1,256]{1,0:T(1,128)} %get-tuple-element.250) | copy-start | bytes 3076
  747.4 423.7 %copy-start.26 = (f32[1,256]{1,0:T(1,128)S(1)}, f32[1,256]{1,0:T(1,128)}, u32[]{:S(2)}) copy-start(f32[1,256]{1,0:T(1,128)} %get-tuple-element.251) | copy-start | bytes 3076
  747.4 423.7 %copy-start.28 = (f32[1,256]{1,0:T(1,128)S(1)}, f32[1,256]{1,0:T(1,128)}, u32[]{:S(2)}) copy-start(f32[1,256]{1,0:T(1,128)} %get-tuple-element.252) | copy-start | bytes 3076
  747.4 423.7 %copy-start.30 = (f32[1,256]{1,0:T(1,128)S(1)}, f32[1,256]{1,0:T(1,128)}, u32[]{:S(2)}) copy-start(f32[1,256]{1,0:T(1,128)} %get-tuple-element.253) | copy-start | bytes 3076
  747.4 423.7 %copy-start.32 = (f32[1,256]{1,0:T(1,128)S(1)}, f32[1,256]{1,0:T(1,128)}, u32[]{:S(2)}) copy-start(f32[1,256]{1,0:T(1,128)} %get-tuple-element.254) | copy-start | bytes 3076
  747.4 423.7 %copy-start.34 = (f32[1,256]{1,0:T(1,128)S(1)}, f32[1,256]{1,0:T(1,128)}, u32[]{:S(2)}) copy-start(f32[1,256]{1,0:T(1,128)} %get-tuple-element.255) | copy-start | bytes 3076
  747.4 423.7 %copy-start.36 = (f32[1,256]{1,0:T(1,128)S(1)}, f32[1,256]{1,0:T(1,128)}, u32[]{:S(2)}) copy-start(f32[1,256]{1,0:T(1,128)} %get-tuple-element.256) | copy-start | bytes 3076
  747.4 423.7 %copy-start.38 = (f32[1,256]{1,0:T(1,128)S(1)}, f32[1,256]{1,0:T(1,128)}, u32[]{:S(2)}) copy-start(f32[1,256]{1,0:T(1,128)} %get-tuple-element.257) | copy-start | bytes 3076
  747.5 423.7 %copy-start.40 = (f32[1,256]{1,0:T(1,128)S(1)}, f32[1,256]{1,0:T(1,128)}, u32[]{:S(2)}) copy-start(f32[1,256]{1,0:T(1,128)} %get-tuple-element.258) | copy-start | bytes 3076
  747.5 423.7 %copy-start.42 = (f32[1,256]{1,0:T(1,128)S(1)}, f32[1,256]{1,0:T(1,128)}, u32[]{:S(2)}) copy-start(f32[1,256]{1,0:T(1,128)} %get-tuple-element.259) | copy-start | bytes 3076
  747.5 423.7 %copy-start.44 = (f32[1,256]{1,0:T(1,128)S(1)}, f32[1,256]{1,0:T(1,128)}, u32[]{:S(2)}) copy-start(f32[1,256]{1,0:T(1,128)} %get-tuple-element.260) | copy-start | bytes 3076
  747.5 423.7 %copy-start.46 = (f32[1,256]{1,0:T(1,128)S(1)}, f32[1,256]{1,0:T(1,128)}, u32[]{:S(2)}) copy-start(f32[1,256]{1,0:T(1,128)} %get-tuple-element.261) | copy-start | bytes 3076
  747.5 423.7 %copy-start.48 = (f32[1,256]{1,0:T(1,128)S(1)}, f32[1,256]{1,0:T(1,128)}, u32[]{:S(2)}) copy-start(f32[1,256]{1,0:T(1,128)} %get-tuple-element.262) | copy-start | bytes 3076
  747.5 423.7 %copy-start.50 = (f32[1,256]{1,0:T(1,128)S(1)}, f32[1,256]{1,0:T(1,128)}, u32[]{:S(2)}) copy-start(f32[1,256]{1,0:T(1,128)} %get-tuple-element.263) | copy-start | bytes 3076
  747.5 423.7 %copy-start.52 = (f32[1,256]{1,0:T(1,128)S(1)}, f32[1,256]{1,0:T(1,128)}, u32[]{:S(2)}) copy-start(f32[1,256]{1,0:T(1,128)} %get-tuple-element.264) | copy-start | bytes 3076
  747.5 423.7 %copy-start.54 = (f32[1,256]{1,0:T(1,128)S(1)}, f32[1,256]{1,0:T(1,128)}, u32[]{:S(2)}) copy-start(f32[1,256]{1,0:T(1,128)} %get-tuple-element.265) | copy-start | bytes 3076
  747.5 423.7 %copy-start.56 = (f32[1,256]{1,0:T(1,128)S(1)}, f32[1,256]{1,0:T(1,128)}, u32[]{:S(2)}) copy-start(f32[1,256]{1,0:T(1,128)} %get-tuple-element.266) | copy-start | bytes 3076
  747.5 423.7 %copy-start.58 = (f32[1,256]{1,0:T(1,128)S(1)}, f32[1,256]{1,0:T(1,128)}, u32[]{:S(2)}) copy-start(f32[1,256]{1,0:T(1,128)} %get-tuple-element.267) | copy-start | bytes 3076
  747.6 423.7 %copy-start.60 = (f32[1,256]{1,0:T(1,128)S(1)}, f32[1,256]{1,0:T(1,128)}, u32[]{:S(2)}) copy-start(f32[1,256]{1,0:T(1,128)} %get-tuple-element.268) | copy-start | bytes 3076
  747.6 423.7 %copy-start.62 = (f32[1,256]{1,0:T(1,128)S(1)}, f32[1,256]{1,0:T(1,128)}, u32[]{:S(2)}) copy-start(f32[1,256]{1,0:T(1,128)} %get-tuple-element.269) | copy-start | bytes 3076
  747.6 423.7 %copy-start.64 = (f32[1,256]{1,0:T(1,128)S(1)}, f32[1,256]{1,0:T(1,128)}, u32[]{:S(2)}) copy-start(f32[1,256]{1,0:T(1,128)} %get-tuple-element.270) | copy-start | bytes 3076
  747.6 423.7 %copy-start.66 = (f32[1,256]{1,0:T(1,128)S(1)}, f32[1,256]{1,0:T(1,128)}, u32[]{:S(2)}) copy-start(f32[1,256]{1,0:T(1,128)} %get-tuple-element.271) | copy-start | bytes 3076
  747.6 423.7 %copy-start.68 = (f32[1,256]{1,0:T(1,128)S(1)}, f32[1,256]{1,0:T(1,128)}, u32[]{:S(2)}) copy-start(f32[1,256]{1,0:T(1,128)} %get-tuple-element.272) | copy-start | bytes 3076
  747.6 423.7 %copy-start.70 = (f32[1,256]{1,0:T(1,128)S(1)}, f32[1,256]{1,0:T(1,128)}, u32[]{:S(2)}) copy-start(f32[1,256]{1,0:T(1,128)} %get-tuple-element.273) | copy-start | bytes 3076
  (98 other events, 165.8 us)
Sparse Core Ops, SparseCore 0:
  162.9 1008.1 all-reduce.6
  1173.9 42.0 all-reduce.8
